TPU v7x, 256 devices: a whole 4x4x8 slice. The times are simulated.
256 devices in a mesh: seg: 4 (over y), bond: 64 (over z, x, core).
Axes of the slice: x: 4, y: 4, z: 8, core: 2. Of those that a mesh axis runs over, the one named last changes fastest.
Arguments:
- sites: float32 [4, 2, 8192, 8192], P('seg', None, 'bond'), may hold values from -0.6629126 to 0.6629126, as said below
- boundary: float32 [8192], P('bond'), may hold values from -6 to 6
- bits: int32 [32, 4], P(None, 'seg'), may hold values from 0 to 1
- order: int32 [32], replicated, may hold values from 0 to 31, each once
Outputs:
- probs: float32 [32, 4], P(None, 'seg')
Inputs may be any that keep to these rules, and one draw needn't show every extreme that they name: `order`: each slot number appears once. `sites`: real entries.
All inputs are finite; a program needn't handle non-finite values.
Results may differ from a plain program's by a relative error of at most 0.0001.
Values sent between devices are 32-bit elements; how exact they have to be, the bound alone decides.
A program may use at most 64 MiB of HBM per device.

v0:
```python
import jax
import jax.numpy as jnp
from jax import lax
from jax.sharding import PartitionSpec as P

D = 8192
ROWS = 32
MB = 32
EPSILON = 1e-06


def shifted(array, axis, by):
    count = lax.axis_size(axis)
    pairs = [(i, i + by) for i in range(count) if 0 <= i + by < count]
    return lax.ppermute(array, axis, pairs)


def advance(site_piece, env_cols, scale, outcome):
    slots = env_cols.shape[1]
    term = jnp.einsum(
        "slr,lm->rsm",
        site_piece,
        env_cols,
        precision=lax.Precision.HIGHEST,
        preferred_element_type=jnp.float32,
    )
    shard = lax.psum_scatter(
        term.reshape(lax.axis_size("bond") * site_piece.shape[1], 2 * slots),
        "bond",
        scatter_dimension=0,
        tiled=True,
    )
    amps = shard.reshape(shard.shape[0], 2, slots)
    local_sq = jnp.sum(amps * amps, axis=0)
    totals = lax.psum(local_sq, "bond")
    means = totals / (D * scale)[None, :] + EPSILON
    picked = outcome == 1
    chosen = jnp.where(picked[None, :], amps[:, 1, :], amps[:, 0, :])
    weight = jnp.where(picked, means[1], means[0])
    probs = weight / (means[0] + means[1])
    env_next = chosen * lax.rsqrt(scale * weight)[None, :]
    scale_next = jnp.ones_like(scale)
    return (env_next, scale_next, probs)


def on_device(sites, boundary, bits, order):
    group = lax.axis_index("seg")
    sections = lax.axis_size("seg")
    block = MB
    count = ROWS // block
    steps = count + sections - 1
    slot_bits = jnp.take(bits, order, axis=0)
    local_width = sites.shape[2]
    start_env = jnp.broadcast_to(boundary[:, None], (local_width, block))
    unit_scale = jnp.ones((block,), jnp.float32)

    def one_step(step, carry):
        env_in, scale_in, table = carry
        batch = step - group
        valid = jnp.logical_and(batch >= 0, batch < count)
        clipped = jnp.clip(batch, 0, count - 1)
        first = group == 0
        env_cols = jnp.where(first, start_env, env_in)
        scale = jnp.where(first, unit_scale, scale_in)
        env_cols, scale, probs = advance(sites[0], env_cols, scale, slot_bits[:, 0])
        columns = [probs]
        block_probs = jnp.stack(columns, axis=1)
        updated = lax.dynamic_update_slice(table, block_probs, (clipped * block, jnp.int32(0)))
        table = jnp.where(valid, updated, table)
        env_out = shifted(env_cols, "seg", 1)
        return (env_out, scale, table)

    table_init = jnp.zeros((ROWS, sites.shape[0]), jnp.float32)
    env_init = jnp.zeros((local_width, block), jnp.float32)
    final = lax.fori_loop(0, steps, one_step, (env_init, unit_scale, table_init))
    return final[2]


def solution(mesh):
    return jax.shard_map(
        on_device,
        mesh=mesh,
        in_specs=(P("seg", None, "bond", None), P("bond"), P(None, "seg"), P()),
        out_specs=P(None, "seg"),
        check_vma=False,
    )
```

profile of v0, /device:TPU:8, one launch (start us, length us, event | category | flops | bytes accessed | tf_op | source)
XLA Modules:
  0.0 1134.0 jit_solution(4633171038704699626)
XLA Ops:
  8.6 1118.4 %while.17 = (s32[]{:T(128)}, f32[128,32]{0,1:T(8,128)S(1)}, f32[32,1]{0,1:T(1,128)S(1)}, s32[32,1]{0,1:T(1,128)S(1)}, pred[]{:T(512)}, /*index=5*/f32[1,2,128,81...) while((s32[]{:T(128)}, f32[128,32]{0,1:T(8,128)S(1)}, f32[32,1]{0,1:T(1,128)S(1)}, ...), condition=%wide.region_4.5_spmd.clone, body=%wide.region_0.4_spmd.clone.sunk | while | flops 805335488 | bytes 17043360 | solution.py:75
  8.6 7.7 fusion.23
  16.4 144.5 %reduce-scatter.2.cloned.1.call-done = f32[128,64]{0,1:T(8,128)} async-done(((f32[8192,64]{0,1:T(8,128)}), f32[128,64]{0,1:T(8,128)}) %reduce-scatter.2.cloned.1.call-update) | async-done | bytes 32784 | tf_op jit(solution)/shard_map/while/body/eval_jaxpr/reduce_scatter | solution.py:27
  160.9 0.9 multiply_reduce_fusion.2
  161.9 124.0 %psum.14 = f32[2,32]{1,0:T(2,128)S(1)} all-reduce(f32[2,32]{1,0:T(2,128)S(1)} %reduce_sum.19), channel_id=1, replica_groups=mesh['seg'=4,'bond'=64] {'bond'}, use_global_device_ids=true, to_apply=%region_3.3 | all-reduce | flops 64 | bytes 512 | tf_op jit(solution)/shard_map/while/body/eval_jaxpr/psum | solution.py:35
  286.7 3.4 collective-permute-start
  290.2 2.2 collective-permute-done
  292.4 7.7 fusion.23
  300.1 139.0 %reduce-scatter.2.cloned.1.call-done = f32[128,64]{0,1:T(8,128)} async-done(((f32[8192,64]{0,1:T(8,128)}), f32[128,64]{0,1:T(8,128)}) %reduce-scatter.2.cloned.1.call-update) | async-done | bytes 32784 | tf_op jit(solution)/shard_map/while/body/eval_jaxpr/reduce_scatter | solution.py:27
  439.1 0.9 multiply_reduce_fusion.2
  440.0 124.0 %psum.14 = f32[2,32]{1,0:T(2,128)S(1)} all-reduce(f32[2,32]{1,0:T(2,128)S(1)} %reduce_sum.19), channel_id=1, replica_groups=mesh['seg'=4,'bond'=64] {'bond'}, use_global_device_ids=true, to_apply=%region_3.3 | all-reduce | flops 64 | bytes 512 | tf_op jit(solution)/shard_map/while/body/eval_jaxpr/psum | solution.py:35
  564.9 3.4 collective-permute-start
  568.4 2.2 collective-permute-done
  570.6 7.7 fusion.23
  578.3 139.0 %reduce-scatter.2.cloned.1.call-done = f32[128,64]{0,1:T(8,128)} async-done(((f32[8192,64]{0,1:T(8,128)}), f32[128,64]{0,1:T(8,128)}) %reduce-scatter.2.cloned.1.call-update) | async-done | bytes 32784 | tf_op jit(solution)/shard_map/while/body/eval_jaxpr/reduce_scatter | solution.py:27
  717.3 0.9 multiply_reduce_fusion.2
  718.3 124.0 %psum.14 = f32[2,32]{1,0:T(2,128)S(1)} all-reduce(f32[2,32]{1,0:T(2,128)S(1)} %reduce_sum.19), channel_id=1, replica_groups=mesh['seg'=4,'bond'=64] {'bond'}, use_global_device_ids=true, to_apply=%region_3.3 | all-reduce | flops 64 | bytes 512 | tf_op jit(solution)/shard_map/while/body/eval_jaxpr/psum | solution.py:35
  843.1 3.4 collective-permute-start
  846.6 2.2 collective-permute-done
  848.8 7.7 fusion.23
  856.5 139.0 %reduce-scatter.2.cloned.1.call-done = f32[128,64]{0,1:T(8,128)} async-done(((f32[8192,64]{0,1:T(8,128)}), f32[128,64]{0,1:T(8,128)}) %reduce-scatter.2.cloned.1.call-update) | async-done | bytes 32784 | tf_op jit(solution)/shard_map/while/body/eval_jaxpr/reduce_scatter | solution.py:27
  996.5 124.0 %psum.14 = f32[2,32]{1,0:T(2,128)S(1)} all-reduce(f32[2,32]{1,0:T(2,128)S(1)} %reduce_sum.19), channel_id=1, replica_groups=mesh['seg'=4,'bond'=64] {'bond'}, use_global_device_ids=true, to_apply=%region_3.3 | all-reduce | flops 64 | bytes 512 | tf_op jit(solution)/shard_map/while/body/eval_jaxpr/psum | solution.py:35
  1121.4 3.4 collective-permute-start
  1124.8 2.2 collective-permute-done
  (43 shorter events, 7.3 us)
Async XLA Ops:
  6.5 0.7 copy-start
  8.6 152.3 %reduce-scatter.2.cloned.1.call-start = ((), (), s32[]{:S(2)}) async-start(), calls=%async_computation.1 | async-start | bytes 2129920 | tf_op jit(solution)/shard_map/while/body/eval_jaxpr/reduce_scatter | solution.py:27
  286.7 5.6 collective-permute-start
  292.4 146.7 %reduce-scatter.2.cloned.1.call-start = ((), (), s32[]{:S(2)}) async-start(), calls=%async_computation.1 | async-start | bytes 2129920 | tf_op jit(solution)/shard_map/while/body/eval_jaxpr/reduce_scatter | solution.py:27
  564.9 5.6 collective-permute-start
  570.5 146.8 %reduce-scatter.2.cloned.1.call-start = ((), (), s32[]{:S(2)}) async-start(), calls=%async_computation.1 | async-start | bytes 2129920 | tf_op jit(solution)/shard_map/while/body/eval_jaxpr/reduce_scatter | solution.py:27
  843.1 5.6 collective-permute-start
  848.8 146.8 %reduce-scatter.2.cloned.1.call-start = ((), (), s32[]{:S(2)}) async-start(), calls=%async_computation.1 | async-start | bytes 2129920 | tf_op jit(solution)/shard_map/while/body/eval_jaxpr/reduce_scatter | solution.py:27
  1121.4 5.6 collective-permute-start
  1127.0 0.5 copy-start.1
Sparse Core Ops, SparseCore 0:
  16.5 144.3 reduce-scatter.1
  300.2 138.8 reduce-scatter.1
  578.4 138.8 reduce-scatter.1
  856.6 138.8 reduce-scatter.1
where the time goes:
time: 1140 us; the launch traced here: 1130 us
  waiting for transfers between devices  570 us (50%)
  blocking collectives  496 us (44%)
  matrix products  30.8 us (3%)
  starting transfers between devices  13.7 us (1%)
  between operations  13.1 us (1%)
    reduce_scatter x4, waiting for transfers between devices, advance(): lax.psum_scatter(term.reshape(lax.axis_size('bond') * site_piece.shape[1]...  562 us
    psum x4, blocking collectives, advance(): totals = lax.psum(local_sq, 'bond')  496 us
    dot_general x4, matrix products, advance(): jnp.einsum('slr,lm->rsm', site_piece, env_cols, precision=lax.Precision.H...  30.8 us
  transfers between devices with their start and end apart: 8, of which 8 were waited for; matrix products, arithmetic and copies ran while one was open for 0% of the time, Pallas kernels for 0%

commit v1 on v0

--- a/solution.py
+++ b/solution.py
@@ -32,7 +32,8 @@
     )
     amps = shard.reshape(shard.shape[0], 2, slots)
     local_sq = jnp.sum(amps * amps, axis=0)
-    totals = lax.psum(local_sq, "bond")
+    parts = lax.all_gather(local_sq, "bond", axis=0, tiled=False)
+    totals = parts.sum(axis=0)
     means = totals / (D * scale)[None, :] + EPSILON
     picked = outcome == 1
     chosen = jnp.where(picked[None, :], amps[:, 1, :], amps[:, 0, :])

time: 1140 us -> 811 us (0.71)
  blocking collectives: 496 us -> 170 us
    psum x4 -> x0, blocking collectives: 496 us -> none  [advance(): totals = lax.psum(local_sq, 'bond')]
    all_gather x0 -> x4, blocking collectives: none -> 170 us  [advance(): parts = lax.all_gather(local_sq, 'bond', axis=0, tiled=False)]
where the time goes in v1:
time: 811 us; the launch traced here: 810 us
  waiting for transfers between devices  573 us (71%)
  blocking collectives  170 us (21%)
  matrix products  30.8 us (4%)
  starting transfers between devices  13.6 us (2%)
  between operations  13.1 us (2%)
  other arithmetic  8.49 us (1%)
    reduce_scatter x4, waiting for transfers between devices, advance(): lax.psum_scatter(term.reshape(lax.axis_size('bond') * site_piece.shape[1]...  564 us
    all_gather x4, blocking collectives, advance(): parts = lax.all_gather(local_sq, 'bond', axis=0, tiled=False)  170 us
    dot_general x4, matrix products, advance(): jnp.einsum('slr,lm->rsm', site_piece, env_cols, precision=lax.Precision.H...  30.8 us
  transfers between devices with their start and end apart: 8, of which 8 were waited for; matrix products, arithmetic and copies ran while one was open for 0% of the time, Pallas kernels for 0%

profile of v1, /device:TPU:8, one launch (start us, length us, event | category | flops | bytes accessed | tf_op | source)
XLA Modules:
  0.0 810.3 jit_solution(9580434429081330187)
XLA Ops:
  8.6 794.6 %while.17 = (s32[]{:T(128)}, f32[128,32]{0,1:T(8,128)S(1)}, f32[32,1]{0,1:T(1,128)S(1)}, s32[32,1]{0,1:T(1,128)S(1)}, pred[]{:T(512)}, /*index=5*/f32[1,2,128,81...) while((s32[]{:T(128)}, f32[128,32]{0,1:T(8,128)S(1)}, ...), condition=%wide.region_4.5_spmd.clone, body=%wide.region_0.4_spmd.clone.sunk | while | flops 805339456 | bytes 17076140 | solution.py:76
  8.6 7.7 fusion.23
  16.4 144.5 %reduce-scatter.2.cloned.1.call-done = f32[128,64]{0,1:T(8,128)} async-done(((f32[8192,64]{0,1:T(8,128)}), f32[128,64]{0,1:T(8,128)}) %reduce-scatter.2.cloned.1.call-update) | async-done | bytes 32784 | tf_op jit(solution)/shard_map/while/body/eval_jaxpr/reduce_scatter | solution.py:27
  160.9 0.9 multiply_reduce_fusion.2
  161.9 42.4 %all_gather.21 = f32[64,2,32]{2,1,0:T(2,128)S(1)} all-gather(f32[1,2,32]{2,1,0:T(2,128)S(1)} %all_gather.20), channel_id=1, replica_groups=mesh['seg'=4,'bond'=64] {'bond'}, dimensions={0}, use_global_device_ids=true | all-gather | bytes 16640 | tf_op jit(solution)/shard_map/while/body/eval_jaxpr/all_gather | solution.py:35
  205.2 3.4 collective-permute-start
  208.6 2.2 collective-permute-done
  210.8 7.7 fusion.23
  218.6 139.8 %reduce-scatter.2.cloned.1.call-done = f32[128,64]{0,1:T(8,128)} async-done(((f32[8192,64]{0,1:T(8,128)}), f32[128,64]{0,1:T(8,128)}) %reduce-scatter.2.cloned.1.call-update) | async-done | bytes 32784 | tf_op jit(solution)/shard_map/while/body/eval_jaxpr/reduce_scatter | solution.py:27
  359.3 42.4 %all_gather.21 = f32[64,2,32]{2,1,0:T(2,128)S(1)} all-gather(f32[1,2,32]{2,1,0:T(2,128)S(1)} %all_gather.20), channel_id=1, replica_groups=mesh['seg'=4,'bond'=64] {'bond'}, dimensions={0}, use_global_device_ids=true | all-gather | bytes 16640 | tf_op jit(solution)/shard_map/while/body/eval_jaxpr/all_gather | solution.py:35
  402.6 3.4 collective-permute-start
  406.0 2.2 collective-permute-done
  408.2 7.7 fusion.23
  416.0 139.9 %reduce-scatter.2.cloned.1.call-done = f32[128,64]{0,1:T(8,128)} async-done(((f32[8192,64]{0,1:T(8,128)}), f32[128,64]{0,1:T(8,128)}) %reduce-scatter.2.cloned.1.call-update) | async-done | bytes 32784 | tf_op jit(solution)/shard_map/while/body/eval_jaxpr/reduce_scatter | solution.py:27
  555.9 0.9 multiply_reduce_fusion.2
  556.8 42.4 %all_gather.21 = f32[64,2,32]{2,1,0:T(2,128)S(1)} all-gather(f32[1,2,32]{2,1,0:T(2,128)S(1)} %all_gather.20), channel_id=1, replica_groups=mesh['seg'=4,'bond'=64] {'bond'}, dimensions={0}, use_global_device_ids=true | all-gather | bytes 16640 | tf_op jit(solution)/shard_map/while/body/eval_jaxpr/all_gather | solution.py:35
  600.1 3.4 collective-permute-start
  603.5 2.2 collective-permute-done
  605.8 7.7 fusion.23
  613.5 139.8 %reduce-scatter.2.cloned.1.call-done = f32[128,64]{0,1:T(8,128)} async-done(((f32[8192,64]{0,1:T(8,128)}), f32[128,64]{0,1:T(8,128)}) %reduce-scatter.2.cloned.1.call-update) | async-done | bytes 32784 | tf_op jit(solution)/shard_map/while/body/eval_jaxpr/reduce_scatter | solution.py:27
  753.3 0.9 multiply_reduce_fusion.2
  754.3 42.4 %all_gather.21 = f32[64,2,32]{2,1,0:T(2,128)S(1)} all-gather(f32[1,2,32]{2,1,0:T(2,128)S(1)} %all_gather.20), channel_id=1, replica_groups=mesh['seg'=4,'bond'=64] {'bond'}, dimensions={0}, use_global_device_ids=true | all-gather | bytes 16640 | tf_op jit(solution)/shard_map/while/body/eval_jaxpr/all_gather | solution.py:35
  797.6 3.4 collective-permute-start
  801.0 2.2 collective-permute-done
  (47 shorter events, 7.6 us)
Async XLA Ops:
  6.5 0.7 copy-start
  8.6 152.3 %reduce-scatter.2.cloned.1.call-start = ((), (), s32[]{:S(2)}) async-start(), calls=%async_computation.1 | async-start | bytes 2129920 | tf_op jit(solution)/shard_map/while/body/eval_jaxpr/reduce_scatter | solution.py:27
  205.2 5.6 collective-permute-start
  210.8 147.5 %reduce-scatter.2.cloned.1.call-start = ((), (), s32[]{:S(2)}) async-start(), calls=%async_computation.1 | async-start | bytes 2129920 | tf_op jit(solution)/shard_map/while/body/eval_jaxpr/reduce_scatter | solution.py:27
  402.6 5.6 collective-permute-start
  408.2 147.6 %reduce-scatter.2.cloned.1.call-start = ((), (), s32[]{:S(2)}) async-start(), calls=%async_computation.1 | async-start | bytes 2129920 | tf_op jit(solution)/shard_map/while/body/eval_jaxpr/reduce_scatter | solution.py:27
  600.1 5.6 collective-permute-start
  605.7 147.6 %reduce-scatter.2.cloned.1.call-start = ((), (), s32[]{:S(2)}) async-start(), calls=%async_computation.1 | async-start | bytes 2129920 | tf_op jit(solution)/shard_map/while/body/eval_jaxpr/reduce_scatter | solution.py:27
  797.6 5.6 collective-permute-start
  803.2 0.5 copy-start.1
Sparse Core Ops, SparseCore 0:
  16.5 144.3 reduce-scatter.1
  218.7 139.6 reduce-scatter.1
  416.1 139.7 reduce-scatter.1
  613.6 139.6 reduce-scatter.1
